TPU v7x, 512 devices: a whole 4x4x16 slice. The times are simulated.
512 devices in a mesh: ep: 16 (over z), mx: 4 (over x), my: 8 (over y, core).
Axes of the slice: x: 4, y: 4, z: 16, core: 2. Of those that a mesh axis runs over, the one named last changes fastest.
Arguments:
- context: bfloat16 [16384, 2048], P(('ep', 'mx')), may hold values from -6 to 6
- resid_in: bfloat16 [16384, 2048], P(('ep', 'mx'), 'my'), may hold values from -70 to 70
- out_weight: bfloat16 [2048, 2048], P(None, 'my'), may hold values from -0.125 to 0.125
- norm_gain: float32 [2048], P('my'), may hold values from 0.5 to 1.5
- gate_weight: bfloat16 [8, 5632, 2048], P(None, ('ep', 'my'), 'mx'), may hold values from -0.125 to 0.125
- up_weight: bfloat16 [8, 5632, 2048], P(None, ('ep', 'my'), 'mx'), may hold values from -0.125 to 0.125
- down_weight: bfloat16 [8, 5632, 2048], P(None, ('ep', 'my'), 'mx'), may hold values from -0.078125 to 0.078125
- routes: int32 [16384, 2], P(('ep', 'mx')), may hold values from 0 to 7, all different within a row; in each aligned block of 256 rows (0 to 255, 256 to 511, ...) at most 96 rows name the same one
- gate_probs: float32 [16384, 2], P(('ep', 'mx')), may hold values from 0.05 to 1
- final_gain: float32 [2048], P('my'), may hold values from 0.5 to 1.5
Outputs:
- normed_out: bfloat16 [16384, 2048], P(('ep', 'mx'), 'my')
- stream_out: bfloat16 [16384, 2048], P(('ep', 'mx'), 'my')
Inputs may be any that keep to these rules, and one draw needn't show every extreme that they name: `routes`: each row names 2 different experts; in each aligned block of 256 rows no expert is named by more than 96 rows, a bound that some block reaches.
All inputs are finite; a program needn't handle non-finite values.
Results may differ from a plain program's by a relative error of at most 0.012.
Values may be sent and summed in bfloat16 or wider, within the bound.
A program may use at most 128 MiB of HBM per device.

v0:
```python
import jax
import jax.numpy as jnp
import numpy as np
from jax import lax
from jax.sharding import PartitionSpec as P

D = 2048
EXPERTS = 8
TOPK = 2
MOST = 96
EPSILON = 1e-06


def row_scale(stream_f):
    partial_sq = jnp.sum(stream_f * stream_f, axis=1)
    row_total = lax.psum(partial_sq, "my")
    return lax.rsqrt(row_total / D + EPSILON)


def shards(
    context,
    resid_in,
    out_weight,
    norm_gain,
    gate_weight,
    up_weight,
    down_weight,
    routes,
    gate_probs,
    final_gain,
):
    ep_count = lax.axis_size("ep")
    slot_dev = max(1, EXPERTS // ep_count)
    slot_total = slot_dev * ep_count
    replicas = slot_total // EXPERTS
    capacity = MOST // replicas
    tok_rows = context.shape[0]
    feat_block = resid_in.shape[1]
    piece_units = gate_weight.shape[1]
    slot_rows = ep_count * capacity
    projected = jnp.dot(context, out_weight, preferred_element_type=jnp.float32)
    stream = (projected + resid_in.astype(jnp.float32)).astype(jnp.bfloat16)
    stream_f = stream.astype(jnp.float32)
    normed = (stream_f * row_scale(stream_f)[:, None] * norm_gain[None, :]).astype(jnp.bfloat16)
    chosen = routes.reshape(-1)
    onehot = (chosen[:, None] == jnp.arange(EXPERTS, dtype=jnp.int32)[None, :]).astype(jnp.int32)
    before = jnp.cumsum(onehot, axis=0) - onehot
    ranking = jnp.sum(before * onehot, axis=1)
    slot_index = chosen * replicas + ranking % replicas
    target = slot_index * capacity + ranking // replicas
    row_ids = jnp.arange(tok_rows * TOPK, dtype=jnp.int32) // TOPK
    source = jnp.full((slot_total * capacity,), tok_rows, jnp.int32).at[target].set(row_ids)
    padded = jnp.concatenate([normed, jnp.zeros((1, feat_block), jnp.bfloat16)], axis=0)
    packed = padded[source].reshape(ep_count, slot_dev, capacity, feat_block)
    landed = lax.all_to_all(packed, "ep", split_axis=0, concat_axis=0, tiled=True)
    gathered = lax.all_gather(landed, "my", axis=3, tiled=True)
    expert_table = (
        np.arange(ep_count)[:, None] * slot_dev + np.arange(slot_dev)[None, :]
    ) // replicas

    def fetch(weight, after):
        chosen_rows, _ = lax.optimization_barrier((weight[expert_table], after))
        got = lax.all_to_all(chosen_rows, "ep", split_axis=0, concat_axis=0, tiled=True)
        wide = lax.all_gather(got, "mx", axis=3, tiled=True)
        return (got, jnp.transpose(wide, (1, 0, 2, 3)).reshape(slot_dev, ep_count * piece_units, D))

    raw_gate, w_gate = fetch(gate_weight, landed)
    raw_up, w_up = fetch(up_weight, raw_gate)
    _, w_down = fetch(down_weight, raw_up)
    tokens_in = jnp.transpose(gathered, (1, 0, 2, 3)).reshape(slot_dev, slot_rows, D)
    gate_proj = jnp.einsum("srd,sfd->srf", tokens_in, w_gate, preferred_element_type=jnp.float32)
    up_proj = jnp.einsum("srd,sfd->srf", tokens_in, w_up, preferred_element_type=jnp.float32)
    hidden = (jax.nn.silu(gate_proj) * up_proj).astype(jnp.bfloat16)
    expert_out = jnp.einsum("srf,sfd->srd", hidden, w_down, preferred_element_type=jnp.float32)
    summed = lax.psum_scatter(
        expert_out.astype(jnp.bfloat16), "my", scatter_dimension=2, tiled=True
    )
    sent_back = summed.reshape(slot_dev, ep_count, capacity, feat_block)
    sent_back = jnp.transpose(sent_back, (1, 0, 2, 3))
    returned = lax.all_to_all(sent_back, "ep", split_axis=0, concat_axis=0, tiled=True).reshape(
        slot_total * capacity, feat_block
    )
    picked = returned[target].reshape(tok_rows, TOPK, feat_block).astype(jnp.float32)
    weights_norm = gate_probs / jnp.sum(gate_probs, axis=1, keepdims=True)
    mixed = jnp.sum(weights_norm[:, :, None] * picked, axis=1)
    updated = stream_f + mixed
    normed_out = (updated * row_scale(updated)[:, None] * final_gain[None, :]).astype(jnp.bfloat16)
    return (normed_out, updated.astype(jnp.bfloat16))


def solution(mesh):
    placed = (
        P(("ep", "mx"), None),
        P(("ep", "mx"), "my"),
        P(None, "my"),
        P("my"),
        P(None, ("ep", "my"), "mx"),
        P(None, ("ep", "my"), "mx"),
        P(None, ("ep", "my"), "mx"),
        P(("ep", "mx"), None),
        P(("ep", "mx"), None),
        P("my"),
    )
    return jax.shard_map(
        shards,
        mesh=mesh,
        in_specs=placed,
        out_specs=(P(("ep", "mx"), "my"), P(("ep", "mx"), "my")),
        check_vma=False,
    )
```

profile of v0, /device:TPU:2, one launch (start us, length us, event | category | flops | bytes accessed | tf_op | source)
XLA Modules:
  0.0 421.2 jit_solution(16044243208929844896)
XLA Ops:
  7.2 0.9 copy.26
  8.4 0.7 broadcast_multiply_fusion
  9.1 1.1 reduce-window.6
  10.9 2.4 scatter_custom_fusion
  13.4 1.7 multiply_reduce_fusion.2
  15.2 15.0 %psum.14 = f32[256]{0:T(256)S(1)} all-reduce(f32[256]{0:T(256)S(1)} %get-tuple-element.10), channel_id=1, replica_groups=mesh['ep'=16,'mx'=4,'my'=8] {'my'}, use_global_device_ids=true, to_apply=%region_2.0 | all-reduce | flops 256 | bytes 2048 | tf_op jit(solution)/shard_map/psum | solution.py:16
  30.3 3.3 gather_fusion
  33.6 15.2 %all-to-all-start = ((bf16[16,1,48,256]{3,2,1,0:T(8,128)(2,1)}), bf16[16,1,48,256]{3,2,1,0:T(8,128)(2,1)S(1)}, u32[]{:S(2)}, u32[]{:S(2)}) async-start(bf16[16,1,48,256]{3,2,1,0:T(8,128)(2,1)} %bitcast.5), calls=%async_computation | async-start | bytes 786432 | tf_op jit(solution)/shard_map/all_to_all | solution.py:55
  48.9 2.6 gather_fusion.1
  51.5 18.3 %all-to-all-done = bf16[16,1,48,256]{3,2,1,0:T(8,128)(2,1)S(1)} async-done(((bf16[16,1,48,256]{3,2,1,0:T(8,128)(2,1)}), bf16[16,1,48,256]{3,2,1,0:T(8,128)(2,1)S(1)}, u32[]{:S(2)}, u32[]{:S(2)}) %all-to-all-start) | async-done | bytes 393248 | tf_op jit(solution)/shard_map/all_to_all | solution.py:55
  70.2 46.5 %all_to_all.25 = bf16[16,1,44,512]{3,2,1,0:T(8,128)(2,1)} all-to-all(bf16[16,1,44,512]{3,2,1,0:T(8,128)(2,1)S(1)} %copy.29), channel_id=1, replica_groups=mesh['ep'=16,'mx'=4,'my'=8] {'ep'}, dimensions={0} | all-to-all | bytes 1441792 | tf_op jit(solution)/shard_map/all_to_all | solution.py:63
  116.8 0.7 all-gather.5.cloned.1.call-update
  117.5 2.6 gather_fusion.2
  120.2 0.4 copy.30
  120.6 46.5 %all_to_all.26 = bf16[16,1,44,512]{3,2,1,0:T(8,128)(2,1)} all-to-all(bf16[16,1,44,512]{3,2,1,0:T(8,128)(2,1)S(1)} %copy.30), channel_id=1, replica_groups=mesh['ep'=16,'mx'=4,'my'=8] {'ep'}, dimensions={0} | all-to-all | bytes 1441792 | tf_op jit(solution)/shard_map/all_to_all | solution.py:63
  167.3 2.6 gather_fusion.3
  170.4 46.6 %all_to_all.27 = bf16[16,1,44,512]{3,2,1,0:T(8,128)(2,1)} all-to-all(bf16[16,1,44,512]{3,2,1,0:T(8,128)(2,1)S(1)} %copy.31), channel_id=1, replica_groups=mesh['ep'=16,'mx'=4,'my'=8] {'ep'}, dimensions={0} | all-to-all | bytes 1441792 | tf_op jit(solution)/shard_map/all_to_all | solution.py:63
  217.1 4.4 %reshape.169 = bf16[704,2048]{1,0:T(8,128)(2,1)} reshape(bf16[16,1,44,2048]{3,2,1,0:T(8,128)(2,1)} %all-gather.7.cloned.1.call-done) | data formatting | bytes 5767168 | tf_op jit(solution)/shard_map/reshape.8
  221.4 6.9 %fusion.14 = f32[768,704]{0,1:T(8,128)} fusion(bf16[768,2048]{1,0:T(8,128)(2,1)} %bitcast.38, bf16[704,2048]{1,0:T(8,128)(2,1)} %reshape.169), kind=kOutput, calls=%fused_computation.50 | convolution fusion | flops 2214592512 | bytes 8192000 | tf_op jit(solution)/shard_map/srd,sfd->srf/dot_general | solution.py:71
  228.3 22.2 %all-gather.9.cloned.1.call-done = bf16[16,1,44,2048]{3,2,1,0:T(8,128)(2,1)} async-done(((bf16[16,1,44,512]{3,2,1,0:T(8,128)(2,1)}), bf16[16,1,44,2048]{3,2,1,0:T(8,128)(2,1)}) %all-gather.9.cloned.1.call-update) | async-done | bytes 2883600 | tf_op jit(solution)/shard_map/all_gather | solution.py:64
  250.6 4.3 %reshape.170 = bf16[704,2048]{1,0:T(8,128)(2,1)} reshape(bf16[16,1,44,2048]{3,2,1,0:T(8,128)(2,1)} %all-gather.9.cloned.1.call-done) | data formatting | bytes 5767168 | tf_op jit(solution)/shard_map/reshape.15
  254.9 45.1 %all-gather.11.cloned.1.call-done = bf16[16,1,44,2048]{3,2,1,0:T(8,128)(2,1)} async-done(((bf16[16,1,44,512]{3,2,1,0:T(8,128)(2,1)}), bf16[16,1,44,2048]{3,2,1,0:T(8,128)(2,1)}) %all-gather.11.cloned.1.call-update) | async-done | bytes 2883600 | tf_op jit(solution)/shard_map/all_gather | solution.py:64
  300.1 4.4 %reshape.171 = bf16[704,2048]{1,0:T(8,128)(2,1)} reshape(bf16[16,1,44,2048]{3,2,1,0:T(8,128)(2,1)} %all-gather.11.cloned.1.call-done) | data formatting | bytes 5767168 | tf_op jit(solution)/shard_map/reshape.18
  304.4 12.4 %fusion = bf16[1,768,2048]{2,1,0:T(8,128)(2,1)} fusion(bf16[704,2048]{1,0:T(8,128)(2,1)} %reshape.171, f32[768,704]{0,1:T(8,128)} %fusion.14, bf16[768,2048]{1,0:T(8,128)(2,1)} %bitcast.39, bf16[704,2048]{1,0:T(8,128)(2,1)} %reshape.170), kind=kOutput, calls=%fused_computation.7 | convolution fusion | flops 4434001920 | bytes 14221312 | tf_op jit(solution)/shard_map/srf,sfd->srd/dot_general | solution.py:74
  316.9 44.6 %reduce-scatter.2.cloned.1.call-done = bf16[1,768,256]{2,1,0:T(8,128)(2,1)} async-done(((bf16[1,768,2048]{2,1,0:T(8,128)(2,1)}), bf16[1,768,256]{2,1,0:T(8,128)(2,1)}) %reduce-scatter.2.cloned.1.call-update) | async-done | bytes 393232 | tf_op jit(solution)/shard_map/reduce_scatter | solution.py:75
  361.5 12.3 %all-to-all-start.4 = ((bf16[16,1,48,256]{3,2,1,0:T(8,128)(2,1)}), bf16[16,1,48,256]{3,2,1,0:T(8,128)(2,1)S(1)}, u32[]{:S(2)}, u32[]{:S(2)}) async-start(bf16[16,1,48,256]{3,2,1,0:T(8,128)(2,1)} %bitcast.34), calls=%async_computation.5 | async-start | bytes 786432 | tf_op jit(solution)/shard_map/all_to_all | solution.py:80
  374.0 20.1 %all-to-all-done.4 = bf16[16,1,48,256]{3,2,1,0:T(8,128)(2,1)S(1)} async-done(((bf16[16,1,48,256]{3,2,1,0:T(8,128)(2,1)}), bf16[16,1,48,256]{3,2,1,0:T(8,128)(2,1)S(1)}, u32[]{:S(2)}, u32[]{:S(2)}) %all-to-all-start.4) | async-done | bytes 393248 | tf_op jit(solution)/shard_map/all_to_all | solution.py:80
  394.1 1.9 gather_fusion.4
  396.3 0.7 multiply_reduce_fusion
  397.0 0.7 fusion.13
  397.8 16.1 %psum.15 = f32[256]{0:T(256)S(1)} all-reduce(f32[256]{0:T(256)S(1)} %multiply_reduce_fusion.1), channel_id=1, replica_groups=mesh['ep'=16,'mx'=4,'my'=8] {'my'}, use_global_device_ids=true, to_apply=%region_10.11 | all-reduce | flops 256 | bytes 2048 | tf_op jit(solution)/shard_map/psum | solution.py:16
  413.9 0.8 multiply_convert_fusion.1
  (55 shorter events, 3.0 us)
Async XLA Ops:
  7.2 6.2 %copy-start = (bf16[256,2048]{1,0:T(8,128)(2,1)S(1)}, bf16[256,2048]{1,0:T(8,128)(2,1)}, u32[]{:S(2)}) copy-start(bf16[256,2048]{1,0:T(8,128)(2,1)} %param.14) | copy-start | bytes 3145732
  7.2 23.0 %copy-start.6 = (f32[256]{0:T(256)S(1)}, f32[256]{0:T(256)}, u32[]{:S(2)}) copy-start(f32[256]{0:T(256)} %param.17) | copy-start | bytes 3076
  15.1 33.7 %copy-start.8 = (s32[16]{0:T(128)S(1)}, s32[16]{0:T(128)}, u32[]{:S(2)}) copy-start(s32[16]{0:T(128)} %constant.78) | copy-start | bytes 196
  15.1 33.7 %copy-start.1 = (bf16[8,44,512]{2,0,1:T(8,128)(2,1)S(1)}, bf16[8,44,512]{2,0,1:T(8,128)(2,1)}, u32[]{:S(2)}) copy-start(bf16[8,44,512]{2,0,1:T(8,128)(2,1)} %param.18) | copy-start | bytes 1081348
  33.6 36.2 %all-to-all-start = ((bf16[16,1,48,256]{3,2,1,0:T(8,128)(2,1)}), bf16[16,1,48,256]{3,2,1,0:T(8,128)(2,1)S(1)}, u32[]{:S(2)}, u32[]{:S(2)}) async-start(bf16[16,1,48,256]{3,2,1,0:T(8,128)(2,1)} %bitcast.5), calls=%async_computation | async-start | bytes 786432 | tf_op jit(solution)/shard_map/all_to_all | solution.py:55
  48.8 168.3 %all-gather.7.cloned.1.call-start = ((), (), s32[]{:S(2)}) async-start(), calls=%async_computation.7 | async-start | bytes 3932160 | tf_op jit(solution)/shard_map/all_gather | solution.py:64
  51.5 66.1 %copy-start.2 = (bf16[8,44,512]{2,0,1:T(8,128)(2,1)S(1)}, bf16[8,44,512]{2,0,1:T(8,128)(2,1)}, u32[]{:S(2)}) copy-start(bf16[8,44,512]{2,0,1:T(8,128)(2,1)} %param.19) | copy-start | bytes 1081348
  69.8 47.0 %copy-start.4 = (bf16[16,1,48,256]{3,2,1,0:T(8,128)(2,1)}, bf16[16,1,48,256]{3,2,1,0:T(8,128)(2,1)S(1)}, u32[]{:S(2)}) copy-start(bf16[16,1,48,256]{3,2,1,0:T(8,128)(2,1)S(1)} %all-to-all-done) | copy-start | bytes 1179652
  116.7 104.7 %all-gather.5.cloned.1.call-start = ((), (), s32[]{:S(2)}) async-start(), calls=%async_computation.6 | async-start | bytes 3538944 | tf_op jit(solution)/shard_map/all_gather | solution.py:56
  117.5 133.1 %all-gather.9.cloned.1.call-start = ((), (), s32[]{:S(2)}) async-start(), calls=%async_computation.8 | async-start | bytes 3932160 | tf_op jit(solution)/shard_map/all_gather | solution.py:64
  120.2 47.2 %copy-start.3 = (bf16[8,44,512]{2,0,1:T(8,128)(2,1)S(1)}, bf16[8,44,512]{2,0,1:T(8,128)(2,1)}, u32[]{:S(2)}) copy-start(bf16[8,44,512]{2,0,1:T(8,128)(2,1)} %param.20) | copy-start | bytes 1081348
  167.1 132.9 %all-gather.11.cloned.1.call-start = ((), (), s32[]{:S(2)}) async-start(), calls=%async_computation.9 | async-start | bytes 3932160 | tf_op jit(solution)/shard_map/all_gather | solution.py:64
  217.0 144.5 %reduce-scatter.2.cloned.1.call-start = ((), (), s32[]{:S(2)}) async-start(), calls=%async_computation.10 | async-start | bytes 3538944 | tf_op jit(solution)/shard_map/reduce_scatter | solution.py:75
  316.9 56.9 %copy-start.5 = (f32[256,2]{0,1:T(2,128)S(1)}, f32[256,2]{0,1:T(2,128)}, u32[]{:S(2)}) copy-start(f32[256,2]{0,1:T(2,128)} %param.22) | copy-start | bytes 6148
  361.5 32.6 %all-to-all-start.4 = ((bf16[16,1,48,256]{3,2,1,0:T(8,128)(2,1)}), bf16[16,1,48,256]{3,2,1,0:T(8,128)(2,1)S(1)}, u32[]{:S(2)}, u32[]{:S(2)}) async-start(bf16[16,1,48,256]{3,2,1,0:T(8,128)(2,1)} %bitcast.34), calls=%async_computation.5 | async-start | bytes 786432 | tf_op jit(solution)/shard_map/all_to_all | solution.py:80
  373.8 40.1 %copy-start.7 = (f32[256]{0:T(256)S(1)}, f32[256]{0:T(256)}, u32[]{:S(2)}) copy-start(f32[256]{0:T(256)} %param.23) | copy-start | bytes 3076
Sparse Core Ops, SparseCore 0:
  116.9 41.5 all-gather.6
  160.6 40.3 all-gather.4
  203.1 47.4 all-gather.8
  252.5 47.4 all-gather.10
  317.0 44.4 reduce-scatter.1
where the time goes:
time: 422 us; the launch traced here: 421 us
  blocking collectives  171 us (41%)
  waiting for transfers between devices  151 us (36%)
  local copies, waits for them, and re-layouts  31.9 us (8%)
  starting transfers between devices  27.9 us (7%)
  matrix products  21.1 us (5%)
  between operations  14.1 us (3%)
  other arithmetic  4.43 us (1%)
    all_to_all x3, blocking collectives, fetch(): lax.all_to_all(chosen_rows, 'ep', split_axis=0, concat_axis=0, tiled=True)  140 us
    all_gather x3, waiting for transfers between devices, fetch(): wide = lax.all_gather(got, 'mx', axis=3, tiled=True)  67.4 us
    reduce_scatter x1, waiting for transfers between devices, shards(): lax.psum_scatter(expert_out.astype(jnp.bfloat16), 'my', scatter_dimension...  44.6 us
    psum x2, blocking collectives, row_scale(): row_total = lax.psum(partial_sq, 'my')  31.1 us
    all_to_all x1, waiting for transfers between devices, shards(): lax.all_to_all(sent_back, 'ep', split_axis=0, concat_axis=0, tiled=True)  20.1 us
    all_to_all x1, waiting for transfers between devices, shards(): lax.all_to_all(packed, 'ep', split_axis=0, concat_axis=0, tiled=True)  18.3 us
    all_to_all x1, starting transfers between devices, shards(): lax.all_to_all(packed, 'ep', split_axis=0, concat_axis=0, tiled=True)  15.2 us
    another operation x4, local copies, waits for them, and re-layouts  13.1 us
  transfers between devices with their start and end apart: 7, of which 5 were waited for; matrix products, arithmetic and copies ran while one was open for 6% of the time, Pallas kernels for 0%

commit v1 on v0

--- a/solution.py
+++ b/solution.py
@@ -3,6 +3,7 @@
 import numpy as np
 from jax import lax
 from jax.sharding import PartitionSpec as P
+from jax.lax import all_to_all, axis_size
 
 D = 2048
 EXPERTS = 8
@@ -61,7 +62,17 @@
     def fetch(weight, after):
         chosen_rows, _ = lax.optimization_barrier((weight[expert_table], after))
         got = lax.all_to_all(chosen_rows, "ep", split_axis=0, concat_axis=0, tiled=True)
-        wide = lax.all_gather(got, "mx", axis=3, tiled=True)
+
+        def edit_map(load, k_dim):
+            seen = []
+            for _ in range(axis_size("mx")):
+                seen.append(load)
+            block_now = jnp.stack(seen, 0)
+            z_new = all_to_all(block_now, axis_name="mx", split_axis=0, concat_axis=0)
+            low = jnp.concatenate(z_new, axis=k_dim)
+            return low
+
+        wide = edit_map(got, 3)
         return (got, jnp.transpose(wide, (1, 0, 2, 3)).reshape(slot_dev, ep_count * piece_units, D))
 
     raw_gate, w_gate = fetch(gate_weight, landed)

time: 422 us -> 455 us (1.078)
  the two profiles are of different devices: /device:TPU:2 before, /device:TPU:6 now
where the time goes in v1:
time: 455 us; the launch traced here: 453 us
  waiting for transfers between devices  261 us (57%)
  starting transfers between devices  73 us (16%)
  local copies, waits for them, and re-layouts  50.1 us (11%)
  blocking collectives  31.8 us (7%)
  matrix products  19 us (4%)
  between operations  14.4 us (3%)
    all_to_all x3, waiting for transfers between devices, fetch(): lax.all_to_all(chosen_rows, 'ep', split_axis=0, concat_axis=0, tiled=True)  110 us
    all_to_all x3, waiting for transfers between devices, edit_map(): z_new = all_to_all(block_now, axis_name='mx', split_axis=0, concat_axis=0)  60.2 us
    reduce_scatter x1, waiting for transfers between devices, shards(): lax.psum_scatter(expert_out.astype(jnp.bfloat16), 'my', scatter_dimension...  51.5 us
    psum x2, blocking collectives, row_scale(): row_total = lax.psum(partial_sq, 'my')  31.8 us
    all_to_all x3, starting transfers between devices, fetch(): lax.all_to_all(chosen_rows, 'ep', split_axis=0, concat_axis=0, tiled=True)  27.1 us
    all_to_all x1, waiting for transfers between devices, shards(): lax.all_to_all(sent_back, 'ep', split_axis=0, concat_axis=0, tiled=True)  20 us
    all_to_all x3, starting transfers between devices, edit_map(): z_new = all_to_all(block_now, axis_name='mx', split_axis=0, concat_axis=0)  18.4 us
    all_to_all x1, waiting for transfers between devices, shards(): lax.all_to_all(packed, 'ep', split_axis=0, concat_axis=0, tiled=True)  18.3 us
  transfers between devices with their start and end apart: 10, of which 9 were waited for; matrix products, arithmetic and copies ran while one was open for 7% of the time, Pallas kernels for 0%

profile of v1, /device:TPU:6, one launch (start us, length us, event | category | flops | bytes accessed | tf_op | source)
XLA Modules:
  0.0 453.5 jit_solution(18324850280351187720)
XLA Ops:
  15.2 15.0 %psum.14 = f32[256]{0:T(256)S(1)} all-reduce(f32[256]{0:T(256)S(1)} %get-tuple-element.10), channel_id=1, replica_groups=mesh['ep'=16,'mx'=4,'my'=8] {'my'}, use_global_device_ids=true, to_apply=%region_2.0 | all-reduce | flops 256 | bytes 2048 | tf_op jit(solution)/shard_map/psum | solution.py:17
  30.3 3.3 gather_fusion
  33.6 15.2 %all-to-all-start = ((bf16[16,1,48,256]{3,2,1,0:T(8,128)(2,1)}), bf16[16,1,48,256]{3,2,1,0:T(8,128)(2,1)S(1)}, u32[]{:S(2)}, u32[]{:S(2)}) async-start(bf16[16,1,48,256]{3,2,1,0:T(8,128)(2,1)} %bitcast.5), calls=%async_computation | async-start | bytes 786432 | tf_op jit(solution)/shard_map/all_to_all | solution.py:56
  48.8 2.6 gather_fusion.1
  51.5 18.3 %all-to-all-done = bf16[16,1,48,256]{3,2,1,0:T(8,128)(2,1)S(1)} async-done(((bf16[16,1,48,256]{3,2,1,0:T(8,128)(2,1)}), bf16[16,1,48,256]{3,2,1,0:T(8,128)(2,1)S(1)}, u32[]{:S(2)}, u32[]{:S(2)}) %all-to-all-start) | async-done | bytes 393248 | tf_op jit(solution)/shard_map/all_to_all | solution.py:56
  71.1 6.5 %all-to-all-start.1 = ((bf16[16,1,44,512]{3,2,1,0:T(8,128)(2,1)}), bf16[16,1,44,512]{3,2,1,0:T(8,128)(2,1)S(1)}, u32[]{:S(2)}, u32[]{:S(2)}) async-start(bf16[16,1,44,512]{3,2,1,0:T(8,128)(2,1)} %copy.44), calls=%async_computation.1 | async-start | bytes 1572864 | tf_op jit(solution)/shard_map/all_to_all | solution.py:64
  77.6 2.6 gather_fusion.2
  80.3 34.9 %all-to-all-done.1 = bf16[16,1,44,512]{3,2,1,0:T(8,128)(2,1)S(1)} async-done(((bf16[16,1,44,512]{3,2,1,0:T(8,128)(2,1)}), bf16[16,1,44,512]{3,2,1,0:T(8,128)(2,1)S(1)}, u32[]{:S(2)}, u32[]{:S(2)}) %all-to-all-start.1) | async-done | bytes 720928 | tf_op jit(solution)/shard_map/all_to_all | solution.py:64
  116.5 8.1 %all-to-all-start.3 = ((bf16[16,1,44,512]{3,2,1,0:T(8,128)(2,1)}), bf16[16,1,44,512]{3,2,1,0:T(8,128)(2,1)S(1)}, u32[]{:S(2)}, u32[]{:S(2)}) async-start(bf16[16,1,44,512]{3,2,1,0:T(8,128)(2,1)} %copy.47), calls=%async_computation.3 | async-start | bytes 1572864 | tf_op jit(solution)/shard_map/all_to_all | solution.py:64
  125.8 38.1 %all-to-all-done.3 = bf16[16,1,44,512]{3,2,1,0:T(8,128)(2,1)S(1)} async-done(((bf16[16,1,44,512]{3,2,1,0:T(8,128)(2,1)}), bf16[16,1,44,512]{3,2,1,0:T(8,128)(2,1)S(1)}, u32[]{:S(2)}, u32[]{:S(2)}) %all-to-all-start.3) | async-done | bytes 720928 | tf_op jit(solution)/shard_map/all_to_all | solution.py:64
  163.8 3.0 stack.6
  166.9 5.2 %all-to-all-start.2 = ((bf16[4,16,1,44,512]{4,1,3,2,0:T(8,128)(2,1)}), bf16[4,16,1,44,512]{4,1,3,2,0:T(8,128)(2,1)}, u32[]{:S(2)}, u32[]{:S(2)}) async-start(bf16[4,16,1,44,512]{4,1,3,2,0:T(8,128)(2,1)} %stack.6), calls=%async_computation.2 | async-start | bytes 5767168 | tf_op jit(solution)/shard_map/all_to_all | solution.py:71
  172.0 2.6 gather_fusion.3
  176.0 24.0 %all-to-all-done.2 = bf16[4,16,1,44,512]{4,1,3,2,0:T(8,128)(2,1)} async-done(((bf16[4,16,1,44,512]{4,1,3,2,0:T(8,128)(2,1)}), bf16[4,16,1,44,512]{4,1,3,2,0:T(8,128)(2,1)}, u32[]{:S(2)}, u32[]{:S(2)}) %all-to-all-start.2) | async-done | bytes 2883616 | tf_op jit(solution)/shard_map/all_to_all | solution.py:71
  200.0 12.5 %all-to-all-start.5 = ((bf16[16,1,44,512]{3,2,1,0:T(8,128)(2,1)}), bf16[16,1,44,512]{3,2,1,0:T(8,128)(2,1)S(1)}, u32[]{:S(2)}, u32[]{:S(2)}) async-start(bf16[16,1,44,512]{3,2,1,0:T(8,128)(2,1)} %copy.50), calls=%async_computation.5 | async-start | bytes 1572864 | tf_op jit(solution)/shard_map/all_to_all | solution.py:64
  213.6 37.1 %all-to-all-done.5 = bf16[16,1,44,512]{3,2,1,0:T(8,128)(2,1)S(1)} async-done(((bf16[16,1,44,512]{3,2,1,0:T(8,128)(2,1)}), bf16[16,1,44,512]{3,2,1,0:T(8,128)(2,1)S(1)}, u32[]{:S(2)}, u32[]{:S(2)}) %all-to-all-start.5) | async-done | bytes 720928 | tf_op jit(solution)/shard_map/all_to_all | solution.py:64
  252.6 6.6 %all-to-all-start.4 = ((bf16[4,16,1,44,512]{4,1,3,2,0:T(8,128)(2,1)}), bf16[4,16,1,44,512]{4,1,3,2,0:T(8,128)(2,1)}, u32[]{:S(2)}, u32[]{:S(2)}) async-start(bf16[4,16,1,44,512]{4,1,3,2,0:T(8,128)(2,1)} %stack.7), calls=%async_computation.4 | async-start | bytes 5767168 | tf_op jit(solution)/shard_map/all_to_all | solution.py:71
  259.7 27.5 %all-to-all-done.4 = bf16[4,16,1,44,512]{4,1,3,2,0:T(8,128)(2,1)} async-done(((bf16[4,16,1,44,512]{4,1,3,2,0:T(8,128)(2,1)}), bf16[4,16,1,44,512]{4,1,3,2,0:T(8,128)(2,1)}, u32[]{:S(2)}, u32[]{:S(2)}) %all-to-all-start.4) | async-done | bytes 2883616 | tf_op jit(solution)/shard_map/all_to_all | solution.py:71
  289.1 6.6 %all-to-all-start.6 = ((bf16[4,16,1,44,512]{4,1,3,2,0:T(8,128)(2,1)}), bf16[4,16,1,44,512]{4,1,3,2,0:T(8,128)(2,1)}, u32[]{:S(2)}, u32[]{:S(2)}) async-start(bf16[4,16,1,44,512]{4,1,3,2,0:T(8,128)(2,1)} %stack.8), calls=%async_computation.6 | async-start | bytes 5767168 | tf_op jit(solution)/shard_map/all_to_all | solution.py:71
  295.7 4.0 copy.46
  299.8 2.5 copy.54
  302.3 5.2 %fusion.14 = f32[768,704]{0,1:T(8,128)S(1)} fusion(bf16[768,2048]{1,0:T(8,128)(2,1)} %bitcast.65, bf16[704,2048]{1,0:T(8,128)(2,1)} %bitcast.59), kind=kOutput, calls=%fused_computation.50 | convolution fusion | flops 2214592512 | bytes 8192000 | tf_op jit(solution)/shard_map/srd,sfd->srf/dot_general | solution.py:82
  307.5 4.0 copy.49
  311.5 2.5 copy.55
  314.0 8.7 %all-to-all-done.6 = bf16[4,16,1,44,512]{4,1,3,2,0:T(8,128)(2,1)} async-done(((bf16[4,16,1,44,512]{4,1,3,2,0:T(8,128)(2,1)}), bf16[4,16,1,44,512]{4,1,3,2,0:T(8,128)(2,1)}, u32[]{:S(2)}, u32[]{:S(2)}) %all-to-all-start.6) | async-done | bytes 2883616 | tf_op jit(solution)/shard_map/all_to_all | solution.py:71
  322.7 4.0 copy.52
  326.7 2.5 copy.56
  329.2 12.0 %fusion = bf16[1,768,2048]{2,1,0:T(8,128)(2,1)} fusion(bf16[704,2048]{1,0:T(8,128)(2,1)} %bitcast.60, f32[768,704]{0,1:T(8,128)S(1)} %fusion.14, bf16[768,2048]{1,0:T(8,128)(2,1)} %bitcast.66, bf16[704,2048]{1,0:T(8,128)(2,1)} %bitcast.58), kind=kOutput, calls=%fused_computation.7 | convolution fusion | flops 4434001920 | bytes 14221312 | tf_op jit(solution)/shard_map/srf,sfd->srd/dot_general | solution.py:85
  341.3 51.5 %reduce-scatter.2.cloned.1.call-done = bf16[1,768,256]{2,1,0:T(8,128)(2,1)} async-done(((bf16[1,768,2048]{2,1,0:T(8,128)(2,1)}), bf16[1,768,256]{2,1,0:T(8,128)(2,1)}) %reduce-scatter.2.cloned.1.call-update) | async-done | bytes 393232 | tf_op jit(solution)/shard_map/reduce_scatter | solution.py:86
  392.8 12.3 %all-to-all-start.7 = ((bf16[16,1,48,256]{3,2,1,0:T(8,128)(2,1)}), bf16[16,1,48,256]{3,2,1,0:T(8,128)(2,1)S(1)}, u32[]{:S(2)}, u32[]{:S(2)}) async-start(bf16[16,1,48,256]{3,2,1,0:T(8,128)(2,1)} %bitcast.61), calls=%async_computation.8 | async-start | bytes 786432 | tf_op jit(solution)/shard_map/all_to_all | solution.py:91
  405.3 20.0 %all-to-all-done.7 = bf16[16,1,48,256]{3,2,1,0:T(8,128)(2,1)S(1)} async-done(((bf16[16,1,48,256]{3,2,1,0:T(8,128)(2,1)}), bf16[16,1,48,256]{3,2,1,0:T(8,128)(2,1)S(1)}, u32[]{:S(2)}, u32[]{:S(2)}) %all-to-all-start.7) | async-done | bytes 393248 | tf_op jit(solution)/shard_map/all_to_all | solution.py:91
  429.1 16.8 %psum.15 = f32[256]{0:T(256)S(1)} all-reduce(f32[256]{0:T(256)S(1)} %multiply_reduce_fusion.1), channel_id=1, replica_groups=mesh['ep'=16,'mx'=4,'my'=8] {'my'}, use_global_device_ids=true, to_apply=%region_10.11 | all-reduce | flops 256 | bytes 2048 | tf_op jit(solution)/shard_map/psum | solution.py:17
  (68 shorter events, 23.3 us)
Async XLA Ops:
  7.2 6.2 %copy-start = (bf16[256,2048]{1,0:T(8,128)(2,1)S(1)}, bf16[256,2048]{1,0:T(8,128)(2,1)}, u32[]{:S(2)}) copy-start(bf16[256,2048]{1,0:T(8,128)(2,1)} %param.14) | copy-start | bytes 3145732
  7.2 23.0 %copy-start.8 = (f32[256]{0:T(256)S(1)}, f32[256]{0:T(256)}, u32[]{:S(2)}) copy-start(f32[256]{0:T(256)} %param.17) | copy-start | bytes 3076
  15.1 15.0 %copy-start.4 = (f32[256,256]{1,0:T(8,128)}, f32[256,256]{1,0:T(8,128)S(1)}, u32[]{:S(2)}) copy-start(f32[256,256]{1,0:T(8,128)S(1)} %get-tuple-element.11) | copy-start | bytes 786436
  15.1 33.6 %copy-start.10 = (s32[16]{0:T(128)S(1)}, s32[16]{0:T(128)}, u32[]{:S(2)}) copy-start(s32[16]{0:T(128)} %constant.78) | copy-start | bytes 196
  15.2 33.7 %copy-start.1 = (bf16[8,44,512]{2,0,1:T(8,128)(2,1)S(1)}, bf16[8,44,512]{2,0,1:T(8,128)(2,1)}, u32[]{:S(2)}) copy-start(bf16[8,44,512]{2,0,1:T(8,128)(2,1)} %param.18) | copy-start | bytes 1081348
  33.6 36.2 %all-to-all-start = ((bf16[16,1,48,256]{3,2,1,0:T(8,128)(2,1)}), bf16[16,1,48,256]{3,2,1,0:T(8,128)(2,1)S(1)}, u32[]{:S(2)}, u32[]{:S(2)}) async-start(bf16[16,1,48,256]{3,2,1,0:T(8,128)(2,1)} %bitcast.5), calls=%async_computation | async-start | bytes 786432 | tf_op jit(solution)/shard_map/all_to_all | solution.py:56
  51.4 26.2 %copy-start.2 = (bf16[8,44,512]{2,0,1:T(8,128)(2,1)S(1)}, bf16[8,44,512]{2,0,1:T(8,128)(2,1)}, u32[]{:S(2)}) copy-start(bf16[8,44,512]{2,0,1:T(8,128)(2,1)} %param.19) | copy-start | bytes 1081348
  69.8 10.5 %copy-start.6 = (bf16[16,1,48,256]{3,2,1,0:T(8,128)(2,1)}, bf16[16,1,48,256]{3,2,1,0:T(8,128)(2,1)S(1)}, u32[]{:S(2)}) copy-start(bf16[16,1,48,256]{3,2,1,0:T(8,128)(2,1)S(1)} %all-to-all-done) | copy-start | bytes 1179652
  71.1 44.1 %all-to-all-start.1 = ((bf16[16,1,44,512]{3,2,1,0:T(8,128)(2,1)}), bf16[16,1,44,512]{3,2,1,0:T(8,128)(2,1)S(1)}, u32[]{:S(2)}, u32[]{:S(2)}) async-start(bf16[16,1,44,512]{3,2,1,0:T(8,128)(2,1)} %copy.44), calls=%async_computation.1 | async-start | bytes 1572864 | tf_op jit(solution)/shard_map/all_to_all | solution.py:64
  116.5 47.4 %all-to-all-start.3 = ((bf16[16,1,44,512]{3,2,1,0:T(8,128)(2,1)}), bf16[16,1,44,512]{3,2,1,0:T(8,128)(2,1)S(1)}, u32[]{:S(2)}, u32[]{:S(2)}) async-start(bf16[16,1,44,512]{3,2,1,0:T(8,128)(2,1)} %copy.47), calls=%async_computation.3 | async-start | bytes 1572864 | tf_op jit(solution)/shard_map/all_to_all | solution.py:64
  166.9 5.2 %copy-start.3 = (bf16[8,44,512]{2,0,1:T(8,128)(2,1)S(1)}, bf16[8,44,512]{2,0,1:T(8,128)(2,1)}, u32[]{:S(2)}) copy-start(bf16[8,44,512]{2,0,1:T(8,128)(2,1)} %param.20) | copy-start | bytes 1081348
  166.9 33.1 %all-to-all-start.2 = ((bf16[4,16,1,44,512]{4,1,3,2,0:T(8,128)(2,1)}), bf16[4,16,1,44,512]{4,1,3,2,0:T(8,128)(2,1)}, u32[]{:S(2)}, u32[]{:S(2)}) async-start(bf16[4,16,1,44,512]{4,1,3,2,0:T(8,128)(2,1)} %stack.6), calls=%async_computation.2 | async-start | bytes 5767168 | tf_op jit(solution)/shard_map/all_to_all | solution.py:71
  200.0 50.7 %all-to-all-start.5 = ((bf16[16,1,44,512]{3,2,1,0:T(8,128)(2,1)}), bf16[16,1,44,512]{3,2,1,0:T(8,128)(2,1)S(1)}, u32[]{:S(2)}, u32[]{:S(2)}) async-start(bf16[16,1,44,512]{3,2,1,0:T(8,128)(2,1)} %copy.50), calls=%async_computation.5 | async-start | bytes 1572864 | tf_op jit(solution)/shard_map/all_to_all | solution.py:64
  212.5 89.8 %all-gather.2.cloned.1.call-start = ((), (), s32[]{:S(2)}) async-start(), calls=%async_computation.9 | async-start | bytes 3538944 | tf_op jit(solution)/shard_map/all_gather | solution.py:57
  252.6 34.5 %all-to-all-start.4 = ((bf16[4,16,1,44,512]{4,1,3,2,0:T(8,128)(2,1)}), bf16[4,16,1,44,512]{4,1,3,2,0:T(8,128)(2,1)}, u32[]{:S(2)}, u32[]{:S(2)}) async-start(bf16[4,16,1,44,512]{4,1,3,2,0:T(8,128)(2,1)} %stack.7), calls=%async_computation.4 | async-start | bytes 5767168 | tf_op jit(solution)/shard_map/all_to_all | solution.py:71
  289.1 33.6 %all-to-all-start.6 = ((bf16[4,16,1,44,512]{4,1,3,2,0:T(8,128)(2,1)}), bf16[4,16,1,44,512]{4,1,3,2,0:T(8,128)(2,1)}, u32[]{:S(2)}, u32[]{:S(2)}) async-start(bf16[4,16,1,44,512]{4,1,3,2,0:T(8,128)(2,1)} %stack.8), calls=%async_computation.6 | async-start | bytes 5767168 | tf_op jit(solution)/shard_map/all_to_all | solution.py:71
  295.7 97.0 %reduce-scatter.2.cloned.1.call-start = ((), (), s32[]{:S(2)}) async-start(), calls=%async_computation.10 | async-start | bytes 3538944 | tf_op jit(solution)/shard_map/reduce_scatter | solution.py:86
  341.3 63.8 %copy-start.7 = (f32[256,2]{0,1:T(2,128)S(1)}, f32[256,2]{0,1:T(2,128)}, u32[]{:S(2)}) copy-start(f32[256,2]{0,1:T(2,128)} %param.22) | copy-start | bytes 6148
  341.3 87.0 %copy-start.5 = (f32[256,256]{1,0:T(8,128)S(1)}, f32[256,256]{1,0:T(8,128)}, u32[]{:S(2)}) copy-start(f32[256,256]{1,0:T(8,128)} %copy-done.4) | copy-start | bytes 786436
  392.8 32.5 %all-to-all-start.7 = ((bf16[16,1,48,256]{3,2,1,0:T(8,128)(2,1)}), bf16[16,1,48,256]{3,2,1,0:T(8,128)(2,1)S(1)}, u32[]{:S(2)}, u32[]{:S(2)}) async-start(bf16[16,1,48,256]{3,2,1,0:T(8,128)(2,1)} %bitcast.61), calls=%async_computation.8 | async-start | bytes 786432 | tf_op jit(solution)/shard_map/all_to_all | solution.py:91
  405.1 40.8 %copy-start.9 = (f32[256]{0:T(256)S(1)}, f32[256]{0:T(256)}, u32[]{:S(2)}) copy-start(f32[256]{0:T(256)} %param.23) | copy-start | bytes 3076
Sparse Core Ops, SparseCore 0:
  215.4 40.9 all-gather.1
  341.4 51.3 reduce-scatter.1
